TPU v7x, 128 devices: a whole 4x4x4 slice. The times are simulated.
128 devices in a mesh: row: 8 (over z_hi, x), blk: 16 (over z_lo, y, core).
Axes of the slice: x: 4, y: 4, z: 4 (z_hi: 2, z_lo: 2; z = z_hi * 2 + z_lo), core: 2. Of those that a mesh axis runs over, the one named last changes fastest.
Arguments:
- spike_counts: int32 [16384, 2048], P(('row', 'blk')), may hold values from 0 to 23, as said below
- kernel_taps: int32 [16], replicated, may hold values from 1 to 8
- lag_bins: int32 [2], replicated, may hold values from 1 to 32, as said below
Outputs:
- correlogram: bfloat16 [2, 16384, 8, 2048], P(None, 'row', None, 'blk')
Inputs may be any that keep to these rules, and one draw needn't show every extreme that they name: `spike_counts`: neurons fire at different rates and share a common drive. `lag_bins`: the second lag equals 32; the first lies between 1 and 31.
All inputs are finite; a program needn't handle non-finite values.
Results may differ from a plain program's by a relative error of at most 0.0034.
Values may be sent and summed in bfloat16 or wider, within the bound.
A program may use at most 128 MiB of HBM per device.

v0:
```python
import jax
import jax.numpy as jnp
from jax import lax
from jax.sharding import PartitionSpec as P

NEURONS = 16384
BINS = 2048
TAPS = 16


def smoothed(spike_counts, kernel_taps):
    counts = spike_counts.astype(jnp.float32)
    weights = kernel_taps.astype(jnp.float32) / jnp.sum(kernel_taps.astype(jnp.float32))
    padded = jnp.pad(counts, ((0, 0), (TAPS - 1, 0)))
    result = jnp.zeros_like(counts)
    for delay in range(TAPS):
        result = result + weights[delay] * padded[:, TAPS - 1 - delay : TAPS - 1 - delay + BINS]
    return result


def later_bins(data, lag):
    padded = jnp.pad(data, ((0, 0), (0, BINS)))
    return lax.dynamic_slice_in_dim(padded, lag, BINS, 1)


def shards(spike_counts, kernel_taps, lag_bins):
    smooth = smoothed(spike_counts, kernel_taps)
    centred = smooth - jnp.mean(smooth, axis=1, keepdims=True)
    totals = lax.psum(jnp.sum(centred, axis=0), ("row", "blk"))
    residual_part = centred - (totals / NEURONS)[None, :]
    zscored = (
        residual_part
        * lax.rsqrt(jnp.mean(residual_part * residual_part, axis=1, keepdims=True) + 1e-05)
    ).astype(jnp.bfloat16)
    span_rows = zscored.shape[0]
    groups = lax.axis_size("row")
    columns = lax.all_gather(zscored, "row", axis=0, tiled=True)
    stacked = jnp.concatenate(
        [later_bins(columns, lag_bins[0]), later_bins(columns, lag_bins[1])], axis=0
    )
    piece = lax.all_gather(zscored, "blk", axis=0, tiled=True)
    product = jnp.dot(piece, stacked.T, preferred_element_type=jnp.float32) / BINS
    product = product.reshape(piece.shape[0], 2, groups, span_rows)
    return jnp.transpose(product, (1, 0, 2, 3)).astype(jnp.bfloat16)


def solution(mesh):
    placed = (P(("row", "blk"), None), P(), P())
    return jax.shard_map(
        shards, mesh=mesh, in_specs=placed, out_specs=P(None, "row", None, "blk"), check_vma=False
    )
```

profile of v0, /device:TPU:1, one launch (start us, length us, event | category | flops | bytes accessed | tf_op | source)
XLA Modules:
  0.0 258.9 jit_solution(15566849793997691235)
XLA Ops:
  6.5 0.0 copy-start
  6.5 0.0 all-gather.5.cloned.1.call-start
  6.5 1.3 convert_reduce_fusion
  7.8 1.3 convert_divide_fusion
  9.1 0.7 fusion.8
  9.8 1.3 convert_element_type.25
  11.2 14.1 %fusion.6 = (f32[128]{0:T(128)S(1)}, f32[128,2048]{1,0:T(8,128)S(1)}) fusion(f32[]{:T(128)} %bitcast.15, f32[]{:T(128)} %bitcast.14, f32[]{:T(128)} %bitcast.13, f32[]{:T(128)} %bitcast.12, f32[]{:T(128)} %bitcast.11, f32[]{:T(128)} %bitcast.10, f32[]{:T(128)} %bitcast.9, f32[]{:T(128)} %bitcast.8, f32[]{:T(128)} %bitcast.7, f32[]{:T(128)} %bitcast.6, ...), kind=kLoop, calls=%fused_computation.19 | loop fusion | flops 8388480 | bytes 2097728 | tf_op jit(solution)/shard_map/reduce_sum | solution.py:28
  25.3 0.2 subtract_reduce_fusion
  25.5 68.7 %psum.7 = f32[2048]{0:T(1024)S(1)} all-reduce(f32[2048]{0:T(1024)S(1)} %subtract_reduce_fusion), channel_id=1, replica_groups=mesh['row'=8,'blk'=16] {'row','blk'}, use_global_device_ids=true, to_apply=%region_3.4 | all-reduce | flops 2048 | bytes 16384 | tf_op jit(solution)/shard_map/psum | solution.py:29
  94.2 0.3 multiply_reduce_fusion
  94.5 1.0 multiply_convert_fusion.1
  95.5 0.0 all-gather.5.cloned.1.call-update
  95.6 0.2 all-gather.3.cloned.1.call-start
  95.8 0.5 all-gather.3.cloned.1.call-update
  96.3 0.0 copy-done
  96.3 0.6 fusion.7
  100.7 62.5 %all-gather.5.cloned.1.call-done = bf16[1024,2048]{1,0:T(8,128)(2,1)} async-done(((bf16[128,2048]{1,0:T(8,128)(2,1)}), bf16[1024,2048]{1,0:T(8,128)(2,1)}) %all-gather.5.cloned.1.call-update) | async-done | bytes 4194320 | tf_op jit(solution)/shard_map/all_gather | solution.py:37
  163.2 10.0 %pad_dynamic-slice_fusion.1 = (bf16[1024,2048]{1,0:T(8,128)(2,1)}, bf16[1024,2048]{1,0:T(8,128)(2,1)}) fusion(s32[]{:T(128)S(6)} %select_n.6, bf16[1024,2048]{1,0:T(8,128)(2,1)} %all-gather.5.cloned.1.call-done, s32[]{:T(128)S(6)} %select_n.7), kind=kLoop, calls=%fused_computation.2 | loop fusion | bytes 12582920 | tf_op jit(solution)/shard_map/dynamic_slice | solution.py:23
  173.2 42.5 %all-gather.3.cloned.1.call-done = bf16[2048,2048]{1,0:T(8,128)(2,1)} async-done(((bf16[128,2048]{1,0:T(8,128)(2,1)}), bf16[2048,2048]{1,0:T(8,128)(2,1)}) %all-gather.3.cloned.1.call-update) | async-done | bytes 8388624 | tf_op jit(solution)/shard_map/all_gather | solution.py:41
  215.7 23.8 %multiply_convert_fusion = bf16[2048,2048]{0,1:T(8,128)(2,1)} fusion(bf16[2048,2048]{1,0:T(8,128)(2,1)} %all-gather.3.cloned.1.call-done, bf16[1024,2048]{1,0:T(8,128)(2,1)} %get-tuple-element.8, bf16[1024,2048]{1,0:T(8,128)(2,1)} %get-tuple-element.7), kind=kOutput, calls=%fused_computation | convolution fusion | flops 17205035008 | bytes 25165824 | tf_op jit(solution)/shard_map/dot_general | solution.py:42
  239.5 12.6 %copy.4 = bf16[2048,2,8,128]{3,2,0,1:T(8,128)(2,1)} copy(bf16[2048,2,8,128]{0,3,2,1:T(8,128)(2,1)} %bitcast.21) | data formatting | bytes 16777216 | tf_op jit(solution)/shard_map/convert_element_type | solution.py:44
  (3 shorter events, 0.0 us)
Async XLA Ops:
  6.5 89.8 %copy-start = (s32[2]{0:T(128)S(1)}, s32[2]{0:T(128)}, u32[]{:S(2)}) copy-start(s32[2]{0:T(128)} %param.5) | copy-start | bytes 28
  6.5 156.7 %all-gather.5.cloned.1.call-start = ((), (), s32[]{:S(2)}) async-start(), calls=%async_computation.1 | async-start | bytes 4718592 | tf_op jit(solution)/shard_map/all_gather | solution.py:37
  95.6 120.2 %all-gather.3.cloned.1.call-start = ((), (), s32[]{:S(2)}) async-start(), calls=%async_computation | async-start | bytes 8912896 | tf_op jit(solution)/shard_map/all_gather | solution.py:41
Sparse Core Ops, SparseCore 0:
  95.7 67.5 all-gather.4
  165.0 50.7 all-gather.2
where the time goes:
time: 260 us; the launch traced here: 259 us
  waiting for transfers between devices  106 us (41%)
  blocking collectives  68.7 us (26%)
  local copies, waits for them, and re-layouts  23.9 us (9%)
  matrix products  23.8 us (9%)
  other arithmetic  19.5 us (8%)
  between operations  17.2 us (7%)
    psum x1, blocking collectives, shards(): totals = lax.psum(jnp.sum(centred, axis=0), ('row', 'blk'))  68.7 us
    all_gather x1, waiting for transfers between devices, shards(): columns = lax.all_gather(zscored, 'row', axis=0, tiled=True)  62.5 us
    all_gather x1, waiting for transfers between devices, shards(): piece = lax.all_gather(zscored, 'blk', axis=0, tiled=True)  42.5 us
    dot_general x1, matrix products, shards(): jnp.dot(piece, stacked.T, preferred_element_type=jnp.float32) / BINS  23.8 us
    reduce_sum x1, other arithmetic, shards(): centred = smooth - jnp.mean(smooth, axis=1, keepdims=True)  14.1 us
    convert_element_type x1, local copies, waits for them, and re-layouts, shards(): return jnp.transpose(product, (1, 0, 2, 3)).astype(jnp.bfloat16)  12.6 us
    dynamic_slice x1, local copies, waits for them, and re-layouts, later_bins(): return lax.dynamic_slice_in_dim(padded, lag, BINS, 1)  9.97 us
  transfers between devices with their start and end apart: 2, of which 2 were waited for; matrix products, arithmetic and copies ran while one was open for 4% of the time, Pallas kernels for 0%

commit v1 on v0

--- a/solution.py
+++ b/solution.py
@@ -26,7 +26,7 @@
 def shards(spike_counts, kernel_taps, lag_bins):
     smooth = smoothed(spike_counts, kernel_taps)
     centred = smooth - jnp.mean(smooth, axis=1, keepdims=True)
-    totals = lax.psum(jnp.sum(centred, axis=0), ("row", "blk"))
+    totals = jnp.sum(lax.all_gather(jnp.sum(centred, axis=0), ("row", "blk")), axis=0)
     residual_part = centred - (totals / NEURONS)[None, :]
     zscored = (
         residual_part

time: 260 us -> 389 us (1.50)
  waiting for transfers between devices: 106 us -> 302 us
  blocking collectives: 68.7 us -> 0 us
    all_gather x0 -> x1, waiting for transfers between devices: none -> 194 us  [shards(): lax.all_gather(jnp.sum(centred, axis=0), ('row', 'blk'))]
    psum x1 -> x0, blocking collectives: 68.7 us -> none  [shards(): totals = lax.psum(jnp.sum(centred, axis=0), ('row', 'blk'))]
  transfers between devices with their start and end apart: 2 -> 3, of which waited for: 2 -> 3; matrix products, arithmetic and copies ran while one was open for 4% -> 3% of each run, Pallas kernels for 0% -> 0%
where the time goes in v1:
time: 389 us; the launch traced here: 388 us
  waiting for transfers between devices  302 us (78%)
  local copies, waits for them, and re-layouts  25.2 us (6%)
  matrix products  23.8 us (6%)
  other arithmetic  20.2 us (5%)
  between operations  16.9 us (4%)
    all_gather x1, waiting for transfers between devices, shards(): lax.all_gather(jnp.sum(centred, axis=0), ('row', 'blk'))  194 us
    all_gather x1, waiting for transfers between devices, shards(): columns = lax.all_gather(zscored, 'row', axis=0, tiled=True)  65 us
    all_gather x1, waiting for transfers between devices, shards(): piece = lax.all_gather(zscored, 'blk', axis=0, tiled=True)  42.5 us
    dot_general x1, matrix products, shards(): jnp.dot(piece, stacked.T, preferred_element_type=jnp.float32) / BINS  23.8 us
    reduce_sum x1, other arithmetic, shards(): centred = smooth - jnp.mean(smooth, axis=1, keepdims=True)  14.1 us
    convert_element_type x1, local copies, waits for them, and re-layouts, shards(): return jnp.transpose(product, (1, 0, 2, 3)).astype(jnp.bfloat16)  12.6 us
    dynamic_slice x1, local copies, waits for them, and re-layouts, later_bins(): return lax.dynamic_slice_in_dim(padded, lag, BINS, 1)  9.97 us
  transfers between devices with their start and end apart: 3, of which 3 were waited for; matrix products, arithmetic and copies ran while one was open for 3% of the time, Pallas kernels for 0%

profile of v1, /device:TPU:1, one launch (start us, length us, event | category | flops | bytes accessed | tf_op | source)
XLA Modules:
  0.0 388.0 jit_solution(17461498117312077280)
XLA Ops:
  6.5 0.0 all-gather.9.cloned.1.call-start
  6.5 1.3 convert_reduce_fusion
  7.8 1.3 convert_divide_fusion
  9.1 0.7 fusion.8
  9.8 1.3 convert_element_type.25
  11.2 14.1 %fusion.6 = (f32[128]{0:T(128)S(1)}, f32[128,2048]{1,0:T(8,128)S(1)}) fusion(f32[]{:T(128)} %bitcast.15, f32[]{:T(128)} %bitcast.14, f32[]{:T(128)} %bitcast.13, f32[]{:T(128)} %bitcast.12, f32[]{:T(128)} %bitcast.11, f32[]{:T(128)} %bitcast.10, f32[]{:T(128)} %bitcast.9, f32[]{:T(128)} %bitcast.8, f32[]{:T(128)} %bitcast.7, f32[]{:T(128)} %bitcast.6, ...), kind=kLoop, calls=%fused_computation.19 | loop fusion | flops 8388480 | bytes 2097728 | tf_op jit(solution)/shard_map/reduce_sum | solution.py:28
  25.3 0.8 subtract_reduce_fusion
  26.1 0.0 all-gather.9.cloned.1.call-update
  26.1 0.0 all-gather.7.cloned.1.call-start
  26.1 193.7 %all-gather.9.cloned.1.call-done = f32[262144]{0:T(1024)} async-done(((f32[2048]{0:T(1024)}), f32[262144]{0:T(1024)}) %all-gather.9.cloned.1.call-update) | async-done | bytes 1048592 | tf_op jit(solution)/shard_map/all_gather | solution.py:29
  219.8 1.4 reshape.17
  221.2 0.1 reduce_sum.48
  221.3 0.3 multiply_reduce_fusion
  221.6 1.0 multiply_convert_fusion.1
  222.6 0.0 all-gather.7.cloned.1.call-update
  222.6 0.2 all-gather.5.cloned.1.call-start
  222.8 0.5 all-gather.5.cloned.1.call-update
  223.4 0.0 copy-done
  223.4 0.6 fusion.7
  227.8 65.0 %all-gather.7.cloned.1.call-done = bf16[1024,2048]{1,0:T(8,128)(2,1)} async-done(((bf16[128,2048]{1,0:T(8,128)(2,1)}), bf16[1024,2048]{1,0:T(8,128)(2,1)}) %all-gather.7.cloned.1.call-update) | async-done | bytes 4194320 | tf_op jit(solution)/shard_map/all_gather | solution.py:37
  292.7 10.0 %pad_dynamic-slice_fusion.1 = (bf16[1024,2048]{1,0:T(8,128)(2,1)}, bf16[1024,2048]{1,0:T(8,128)(2,1)}) fusion(s32[]{:T(128)S(6)} %select_n.6, bf16[1024,2048]{1,0:T(8,128)(2,1)} %all-gather.7.cloned.1.call-done, s32[]{:T(128)S(6)} %select_n.7), kind=kLoop, calls=%fused_computation.2 | loop fusion | bytes 12582920 | tf_op jit(solution)/shard_map/dynamic_slice | solution.py:23
  302.7 42.5 %all-gather.5.cloned.1.call-done = bf16[2048,2048]{1,0:T(8,128)(2,1)} async-done(((bf16[128,2048]{1,0:T(8,128)(2,1)}), bf16[2048,2048]{1,0:T(8,128)(2,1)}) %all-gather.5.cloned.1.call-update) | async-done | bytes 8388624 | tf_op jit(solution)/shard_map/all_gather | solution.py:41
  345.2 23.8 %multiply_convert_fusion = bf16[2048,2048]{0,1:T(8,128)(2,1)} fusion(bf16[2048,2048]{1,0:T(8,128)(2,1)} %all-gather.5.cloned.1.call-done, bf16[1024,2048]{1,0:T(8,128)(2,1)} %get-tuple-element.8, bf16[1024,2048]{1,0:T(8,128)(2,1)} %get-tuple-element.7), kind=kOutput, calls=%fused_computation | convolution fusion | flops 17205035008 | bytes 25165824 | tf_op jit(solution)/shard_map/dot_general | solution.py:42
  369.0 12.6 %copy.6 = bf16[2048,2,8,128]{3,2,0,1:T(8,128)(2,1)} copy(bf16[2048,2,8,128]{0,3,2,1:T(8,128)(2,1)} %bitcast.21) | data formatting | bytes 16777216 | tf_op jit(solution)/shard_map/convert_element_type | solution.py:44
  (4 shorter events, 0.0 us)
Async XLA Ops:
  6.5 216.8 %copy-start = (s32[2]{0:T(128)S(1)}, s32[2]{0:T(128)}, u32[]{:S(2)}) copy-start(s32[2]{0:T(128)} %param.5) | copy-start | bytes 28
  6.5 213.3 %all-gather.9.cloned.1.call-start = ((), (), s32[]{:S(2)}) async-start(), calls=%async_computation.2 | async-start | bytes 1056768 | tf_op jit(solution)/shard_map/all_gather | solution.py:29
  26.1 266.7 %all-gather.7.cloned.1.call-start = ((), (), s32[]{:S(2)}) async-start(), calls=%async_computation.1 | async-start | bytes 4718592 | tf_op jit(solution)/shard_map/all_gather | solution.py:37
  222.6 122.6 %all-gather.5.cloned.1.call-start = ((), (), s32[]{:S(2)}) async-start(), calls=%async_computation | async-start | bytes 8912896 | tf_op jit(solution)/shard_map/all_gather | solution.py:41
Sparse Core Ops, SparseCore 0:
  26.2 193.5 all-gather.8
  222.7 69.9 all-gather.6
  294.4 50.7 all-gather.4
